TPU v7x, 128 devices: a whole 4x4x4 slice. The times are simulated.
128 devices in a mesh: rows: 32 (over x, z, core), cols: 4 (over y).
Axes of the slice: x: 4, y: 4, z: 4, core: 2. Of those that a mesh axis runs over, the one named last changes fastest.
Arguments:
- points: float32 [98304, 1024], P('rows', 'cols'), may hold values from -80 to 80
- codes: int32 [128, 98304], P('cols', 'rows'), may hold values from 0 to 255, as said below
- rotation: float32 [1024, 1024], P('rows', 'cols'), may hold values from -0.16 to 1.16
Outputs:
- new_rotation: float32 [1024, 1024], P('rows', 'cols')
- centroids: float32 [128, 2048], P('cols')
Inputs may be any that keep to these rules, and one draw needn't show every extreme that they name: For every subspace, the first 256 vectors hold each of the 256 codes once.
All inputs are finite; a program needn't handle non-finite values.
Results may differ from a plain program's by a relative error of at most 0.00011.
Values sent between devices are 32-bit elements; how exact they have to be, the bound alone decides.
No kernel may reach another device: no remote copies, remote signals or barrier semaphores. Data moves between devices by JAX's collectives and lax.ppermute only.
A program may use at most 128 MiB of HBM per device.

v0:
```python
import jax
import jax.numpy as jnp
from jax import lax
from jax.sharding import PartitionSpec as P

D = 1024
K = 256
NS_ITERS = 6
SUB = 8


def contract_rows(left, right):
    return lax.dot_general(
        left,
        right,
        (((0,), (0,)), ((), ())),
        precision=lax.Precision.HIGHEST,
        preferred_element_type=jnp.float32,
    )


def matmul_high(left, right):
    return jnp.dot(left, right, precision=lax.Precision.HIGHEST, preferred_element_type=jnp.float32)


def gram_parts(current):
    row_block = lax.all_gather(current, "cols", axis=1, tiled=True)
    partial_gram = contract_rows(row_block, current)
    return (row_block, lax.psum(partial_gram, "rows"))


def shards(points, codes, rotation):
    gathered = lax.all_gather(points, "cols", axis=1, tiled=True)
    column_panel = lax.all_gather(rotation, "rows", axis=0, tiled=True)
    rotated = matmul_high(gathered, column_panel)
    local_subspaces = codes.shape[0]
    vector_count = rotated.shape[0]
    panel_width = rotated.shape[1]
    batch_size = 4
    turn_count = local_subspaces // batch_size
    code_range = jnp.arange(K, dtype=jnp.int32)
    rotated_groups = rotated.reshape(vector_count, turn_count, batch_size, SUB).transpose(
        1, 2, 0, 3
    )
    code_groups = codes.reshape(turn_count, batch_size, vector_count)

    def local_totals(carry, item):
        block_values, code_block = item
        indicator = (code_block[:, :, None] == code_range[None, None, :]).astype(jnp.float32)
        value_sums = jnp.einsum(
            "gnk,gns->gks",
            indicator,
            block_values,
            precision=lax.Precision.HIGHEST,
            preferred_element_type=jnp.float32,
        )
        return (carry, (value_sums, jnp.sum(indicator, axis=1)))

    unused, (value_totals, code_totals) = lax.scan(local_totals, 0.0, (rotated_groups, code_groups))
    value_totals = value_totals.reshape(local_subspaces, K * SUB)
    code_totals = code_totals.reshape(local_subspaces, K)
    owned_values, owned_counts = (
        lax.psum_scatter(value_totals, "rows", scatter_dimension=0, tiled=True),
        lax.psum_scatter(code_totals, "rows", scatter_dimension=0, tiled=True),
    )
    owned_centers = (owned_values.reshape(-1, K, SUB) / owned_counts[:, :, None]).reshape(
        -1, K * SUB
    )
    centroids = lax.all_gather(owned_centers, "rows", axis=0, tiled=True)
    center_groups = centroids.reshape(turn_count, batch_size, K, SUB)

    def rebuild(carry, item):
        code_block, center_block = item
        indicator = (code_block[:, :, None] == code_range[None, None, :]).astype(jnp.float32)
        return (
            carry,
            jnp.einsum(
                "gnk,gks->gns",
                indicator,
                center_block,
                precision=lax.Precision.HIGHEST,
                preferred_element_type=jnp.float32,
            ),
        )

    unused, rebuilt = lax.scan(rebuild, 0.0, (code_groups, center_groups))
    approx = rebuilt.transpose(2, 0, 1, 3).reshape(vector_count, panel_width)
    cross_block = lax.psum_scatter(
        contract_rows(gathered, approx), "rows", scatter_dimension=0, tiled=True
    )
    square_total = lax.psum(jnp.sum(cross_block * cross_block), ("rows", "cols"))
    iterate = 1.7 * cross_block / jnp.sqrt(square_total + 1e-06)
    for step_index in range(NS_ITERS):
        row_block, gram_panel = gram_parts(iterate)
        iterate = 1.5 * iterate - 0.5 * matmul_high(row_block, gram_panel)
    return (iterate * D**0.5, centroids)


def solution(mesh):
    in_specs = (P("rows", "cols"), P("cols", "rows"), P("rows", "cols"))
    out_specs = (P("rows", "cols"), P("cols", None))
    return jax.shard_map(shards, mesh=mesh, in_specs=in_specs, out_specs=out_specs, check_vma=False)
```

profile of v0, /device:TPU:6, one launch (start us, length us, event | category | flops | bytes accessed | tf_op | source)
XLA Modules:
  0.0 1367.0 jit_solution(11022926561968581953)
XLA Ops:
  8.9 46.3 %all-gather.6.cloned.1.call-done = f32[1024,256]{1,0:T(8,128)} async-done(((f32[32,256]{1,0:T(8,128)}), f32[1024,256]{1,0:T(8,128)}) %all-gather.6.cloned.1.call-update) | async-done | bytes 1048592 | tf_op jit(solution)/shard_map/all_gather | solution.py:34
  55.2 119.8 %all-gather.4.cloned.1.call-done = f32[3072,1024]{1,0:T(8,128)} async-done(((f32[3072,256]{1,0:T(8,128)}), f32[3072,1024]{1,0:T(8,128)}) %all-gather.4.cloned.1.call-update) | async-done | bytes 12582928 | tf_op jit(solution)/shard_map/all_gather | solution.py:33
  175.0 13.8 %fusion.28 = f32[3072,256]{0,1:T(8,128)S(1)} fusion(f32[3072,1024]{1,0:T(8,128)} %all-gather.4.cloned.1.call-done, f32[1024,256]{1,0:T(8,128)} %all-gather.6.cloned.1.call-done), kind=kOutput, calls=%fused_computation.43 | convolution fusion | flops 9663676416 | bytes 16777216 | tf_op jit(solution)/shard_map/dot_general | solution.py:23
  188.8 63.4 %while.24 = (s32[]{:T(128)}, f32[8,4,256,8]{2,3,1,0:T(8,128)}, f32[8,4,256]{2,1,0:T(4,128)}, s32[8,4,3072]{2,1,0:T(4,128)S(1)}, f32[8,4,3072,8]{2,3,1,0:T(8,128)S(1)}, /*index=5*/s32[]{:T(128)}) while((s32[]{:T(128)}, f32[8,4,256,8]{2,3,1,0:T(8,128)}, f32[8,4,256]{2,1,0:T(4,128)}, s32[8,4,3072]{2,1,0:T(4,128)S(1)}, ...), condition=%wide.region_2.3_spmd.clone, body=%wide.region_0.2_spmd.clone.sunk | while | flops 314571776 | bytes 636489 | solution.py:59
  188.9 5.1 fusion.69
  193.9 2.3 fusion.70
  196.8 5.0 fusion.69
  201.8 2.3 fusion.70
  204.7 5.0 fusion.69
  209.8 2.3 fusion.70
  212.6 5.0 fusion.69
  217.7 2.3 fusion.70
  220.6 5.0 fusion.69
  225.6 2.3 fusion.70
  228.5 5.0 fusion.69
  233.5 2.3 fusion.70
  236.4 5.0 fusion.69
  241.4 2.3 fusion.70
  244.3 5.0 fusion.69
  249.4 2.3 fusion.70
  252.2 3.5 copy.22
  255.7 4.7 reshape.46
  261.9 109.6 %all-reduce.1 = f32[32,256]{1,0:T(8,128)S(1)} all-reduce(f32[32,256]{1,0:T(8,128)S(1)} %reshape.47), channel_id=3, replica_groups=mesh['rows'=32,'cols'=4] {'rows'}, use_global_device_ids=true, to_apply=%region_4.5.clone | all-reduce | flops 8192 | bytes 65536
  372.5 1.5 fusion.27
  374.1 41.1 %all-gather = f32[32,1,2048]{2,1,0:T(1,128)S(1)} all-gather(f32[1,1,2048]{2,1,0:T(1,128)S(1)} %fusion.27), channel_id=1, replica_groups=mesh['rows'=32,'cols'=4] {'rows'}, dimensions={0}, use_global_device_ids=true | all-gather | bytes 270336 | tf_op jit(solution)/shard_map/all_gather | solution.py:69
  415.7 3.7 reshape.48
  419.4 2.8 copy.23
  422.2 59.3 %while.25 = (s32[]{:T(128)}, f32[8,4,3072,8]{2,3,1,0:T(8,128)}, s32[8,4,3072]{2,1,0:T(4,128)S(1)}, f32[8,4,256,8]{2,3,1,0:T(8,128)S(1)}, s32[]{:T(128)}) while((s32[]{:T(128)}, f32[8,4,3072,8]{2,3,1,0:T(8,128)}, s32[8,4,3072]{2,1,0:T(4,128)S(1)}, f32[8,4,256,8]{2,3,1,0:T(8,128)S(1)}, s32[]{:T(128)}) %tuple.73), condition=%wide.region_6.7_spmd.clone, body=%wide.region_5.6_spmd.clone.sunk | while | flops 305135616 | bytes 574529 | solution.py:86
  422.2 7.4 fusion.72
  429.6 7.4 fusion.72
  437.0 7.4 fusion.72
  444.4 7.4 fusion.72
  451.8 7.4 fusion.72
  459.2 7.4 fusion.72
  466.6 7.4 fusion.72
  474.0 7.4 fusion.72
  481.4 13.6 convolution_bitcast_fusion
  495.1 1.3 copy.25
  496.5 76.6 %reduce-scatter.4.cloned.1.call-done = f32[32,256]{1,0:T(8,128)} async-done(((f32[1024,256]{1,0:T(8,128)}), f32[32,256]{1,0:T(8,128)}) %reduce-scatter.4.cloned.1.call-update) | async-done | bytes 32784 | tf_op jit(solution)/shard_map/reduce_scatter | solution.py:88
  574.6 62.3 %psum.49 = f32[]{:T(128)} all-reduce(f32[]{:T(128)} %multiply_reduce_fusion), channel_id=1, replica_groups=mesh['rows'=32,'cols'=4] {'rows','cols'}, use_global_device_ids=true, to_apply=%region_9.10 | all-reduce | flops 1 | bytes 8 | tf_op jit(solution)/shard_map/psum | solution.py:91
  638.3 12.0 all_gather.30
  650.3 2.1 fusion.29
  652.4 105.1 %all-reduce.10.cloned.1.call-done = f32[1024,256]{1,0:T(8,128)} async-done(((f32[1024,256]{1,0:T(8,128)}), f32[1024,256]{1,0:T(8,128)}) %all-reduce.10.cloned.1.call-update) | async-done | bytes 1048592 | tf_op jit(solution)/shard_map/psum | solution.py:29
  757.6 1.8 fusion.26
  759.4 12.4 all_gather.31
  771.8 2.1 fusion.30
  773.9 103.6 %all-reduce.12.cloned.1.call-done = f32[1024,256]{1,0:T(8,128)} async-done(((f32[1024,256]{1,0:T(8,128)}), f32[1024,256]{1,0:T(8,128)}) %all-reduce.12.cloned.1.call-update) | async-done | bytes 1048592 | tf_op jit(solution)/shard_map/psum | solution.py:29
  877.5 1.8 fusion.25
  879.4 12.6 all_gather.32
  892.0 2.1 fusion.31
  894.1 103.7 %all-reduce.14.cloned.1.call-done = f32[1024,256]{1,0:T(8,128)} async-done(((f32[1024,256]{1,0:T(8,128)}), f32[1024,256]{1,0:T(8,128)}) %all-reduce.14.cloned.1.call-update) | async-done | bytes 1048592 | tf_op jit(solution)/shard_map/psum | solution.py:29
  997.8 1.8 fusion.24
  999.6 12.4 all_gather.33
  1012.0 2.1 fusion.32
  1014.1 103.7 %all-reduce.16.cloned.1.call-done = f32[1024,256]{1,0:T(8,128)} async-done(((f32[1024,256]{1,0:T(8,128)}), f32[1024,256]{1,0:T(8,128)}) %all-reduce.16.cloned.1.call-update) | async-done | bytes 1048592 | tf_op jit(solution)/shard_map/psum | solution.py:29
  1117.8 1.8 fusion.23
  1119.6 12.4 all_gather.34
  1132.0 2.1 fusion.33
  1134.1 103.7 %all-reduce.18.cloned.1.call-done = f32[1024,256]{1,0:T(8,128)} async-done(((f32[1024,256]{1,0:T(8,128)}), f32[1024,256]{1,0:T(8,128)}) %all-reduce.18.cloned.1.call-update) | async-done | bytes 1048592 | tf_op jit(solution)/shard_map/psum | solution.py:29
  1237.8 1.8 fusion.22
  1239.6 12.4 all_gather.35
  1252.0 2.1 fusion.34
  1254.8 102.9 %all-reduce.20.cloned.1.call-done = f32[1024,256]{1,0:T(8,128)} async-done(((f32[1024,256]{1,0:T(8,128)}), f32[1024,256]{1,0:T(8,128)}) %all-reduce.20.cloned.1.call-update) | async-done | bytes 1048592 | tf_op jit(solution)/shard_map/psum | solution.py:29
  1357.7 2.4 fusion.21
  (63 shorter events, 12.9 us)
Async XLA Ops:
  7.2 1.6 copy-start
  7.2 48.0 %all-gather.6.cloned.1.call-start = ((), (), s32[]{:S(2)}) async-start(), calls=%async_computation.2 | async-start | bytes 1081344 | tf_op jit(solution)/shard_map/all_gather | solution.py:34
  7.9 167.1 %all-gather.4.cloned.1.call-start = ((), (), s32[]{:S(2)}) async-start(), calls=%async_computation.1 | async-start | bytes 15728640 | tf_op jit(solution)/shard_map/all_gather | solution.py:33
  8.7 363.8 %all-reduce.22.cloned.1.call-start = ((), (), s32[]{:S(2)}) async-start(), calls=%async_computation.10 | async-start | bytes 524288
  255.7 4.8 copy-start.1
  260.4 312.7 %reduce-scatter.4.cloned.1.call-start = ((), (), s32[]{:S(2)}) async-start(), calls=%async_computation.9 | async-start | bytes 1081344 | tf_op jit(solution)/shard_map/reduce_scatter | solution.py:88
  496.4 261.1 %all-reduce.10.cloned.1.call-start = ((), (), s32[]{:S(2)}) async-start(), calls=%async_computation.3 | async-start | bytes 2097152 | tf_op jit(solution)/shard_map/psum | solution.py:29
  652.4 225.2 %all-reduce.12.cloned.1.call-start = ((), (), s32[]{:S(2)}) async-start(), calls=%async_computation.4 | async-start | bytes 2097152 | tf_op jit(solution)/shard_map/psum | solution.py:29
  773.8 223.9 %all-reduce.14.cloned.1.call-start = ((), (), s32[]{:S(2)}) async-start(), calls=%async_computation.5 | async-start | bytes 2097152 | tf_op jit(solution)/shard_map/psum | solution.py:29
  894.1 223.7 %all-reduce.16.cloned.1.call-start = ((), (), s32[]{:S(2)}) async-start(), calls=%async_computation.6 | async-start | bytes 2097152 | tf_op jit(solution)/shard_map/psum | solution.py:29
  1014.1 223.7 %all-reduce.18.cloned.1.call-start = ((), (), s32[]{:S(2)}) async-start(), calls=%async_computation.7 | async-start | bytes 2097152 | tf_op jit(solution)/shard_map/psum | solution.py:29
  1134.0 223.7 %all-reduce.20.cloned.1.call-start = ((), (), s32[]{:S(2)}) async-start(), calls=%async_computation.8 | async-start | bytes 2097152 | tf_op jit(solution)/shard_map/psum | solution.py:29
Sparse Core Ops, SparseCore 0:
  10.3 44.8 all-gather.5
  56.8 118.0 all-gather.3
  260.5 103.2 all-reduce.21
  496.5 76.4 reduce-scatter.3
  652.5 105.0 all-reduce.9
  774.0 103.5 all-reduce.11
  894.2 103.5 all-reduce.13
  1014.2 103.5 all-reduce.15
  1134.2 103.5 all-reduce.17
  1254.2 103.5 all-reduce.19
where the time goes:
time: 1370 us
  waiting for transfers between devices  867 us (63%)
  blocking collectives  287 us (21%)
  matrix products  151 us (11%)
  local copies, waits for them, and re-layouts  24.9 us (2%)
  other arithmetic  21.8 us (2%)
  between operations  15 us (1%)
    psum x6, waiting for transfers between devices, gram_parts(): return (row_block, lax.psum(partial_gram, 'rows'))  623 us
    all_gather x1, waiting for transfers between devices, shards(): gathered = lax.all_gather(points, 'cols', axis=1, tiled=True)  120 us
    unnamed x1, blocking collectives  110 us
    reduce_scatter x1, waiting for transfers between devices, shards(): lax.psum_scatter(contract_rows(gathered, approx), 'rows', scatter_dimensi...  76.6 us
    all_gather x6, blocking collectives, gram_parts(): row_block = lax.all_gather(current, 'cols', axis=1, tiled=True)  74.1 us
    psum x1, blocking collectives, shards(): lax.psum(jnp.sum(cross_block * cross_block), ('rows', 'cols'))  62.3 us
    dot_general x8, matrix products, rebuild(): jnp.einsum('gnk,gks->gns', indicator, center_block, precision=lax.Precisi...  59.2 us
    all_gather x1, waiting for transfers between devices, shards(): column_panel = lax.all_gather(rotation, 'rows', axis=0, tiled=True)  46.3 us
  transfers between devices with their start and end apart: 10, of which 9 were waited for; matrix products, arithmetic and copies ran while one was open for 0% of the time, Pallas kernels for 0%

commit v1 on v0

--- a/solution.py
+++ b/solution.py
@@ -26,7 +26,7 @@
 def gram_parts(current):
     row_block = lax.all_gather(current, "cols", axis=1, tiled=True)
     partial_gram = contract_rows(row_block, current)
-    return (row_block, lax.psum(partial_gram, "rows"))
+    return (row_block, jnp.sum(lax.all_gather(partial_gram, "rows"), axis=0))
 
 
 def shards(points, codes, rotation):

time: 1370 us -> 1490 us (1.088)
  other arithmetic: 21.8 us -> 93.4 us
  waiting for transfers between devices: 867 us -> 920 us
    all_gather x0 -> x6, waiting for transfers between devices: none -> 676 us  [gram_parts(): return (row_block, jnp.sum(lax.all_gather(partial_gram, 'rows'), axis=0))]
    psum x6 -> x0, waiting for transfers between devices: 623 us -> none  [gram_parts(): return (row_block, lax.psum(partial_gram, 'rows'))]
    reduce_sum x0 -> x6, other arithmetic: none -> 71.6 us  [gram_parts(): return (row_block, jnp.sum(lax.all_gather(partial_gram, 'rows'), axis=0))]
where the time goes in v1:
time: 1490 us; the launch traced here: 1480 us
  waiting for transfers between devices  920 us (62%)
  blocking collectives  287 us (19%)
  matrix products  143 us (10%)
  other arithmetic  93.4 us (6%)
  local copies, waits for them, and re-layouts  25.1 us (2%)
  between operations  15.1 us (1%)
    all_gather x6, waiting for transfers between devices, gram_parts(): return (row_block, jnp.sum(lax.all_gather(partial_gram, 'rows'), axis=0))  676 us
    all_gather x1, waiting for transfers between devices, shards(): gathered = lax.all_gather(points, 'cols', axis=1, tiled=True)  120 us
    unnamed x1, blocking collectives  110 us
    reduce_scatter x1, waiting for transfers between devices, shards(): lax.psum_scatter(contract_rows(gathered, approx), 'rows', scatter_dimensi...  76.6 us
    all_gather x6, blocking collectives, gram_parts(): row_block = lax.all_gather(current, 'cols', axis=1, tiled=True)  73.7 us
    reduce_sum x6, other arithmetic, gram_parts(): return (row_block, jnp.sum(lax.all_gather(partial_gram, 'rows'), axis=0))  71.6 us
    psum x1, blocking collectives, shards(): lax.psum(jnp.sum(cross_block * cross_block), ('rows', 'cols'))  62.3 us
    dot_general x8, matrix products, rebuild(): jnp.einsum('gnk,gks->gns', indicator, center_block, precision=lax.Precisi...  59.2 us
  transfers between devices with their start and end apart: 10, of which 9 were waited for; matrix products, arithmetic and copies ran while one was open for 0% of the time, Pallas kernels for 0%

profile of v1, /device:TPU:6, one launch (start us, length us, event | category | flops | bytes accessed | tf_op | source)
XLA Modules:
  0.0 1483.6 jit_solution(13443713318558839122)
XLA Ops:
  9.8 45.4 %all-gather.18.cloned.1.call-done = f32[1024,256]{1,0:T(8,128)} async-done(((f32[32,256]{1,0:T(8,128)}), f32[1024,256]{1,0:T(8,128)}) %all-gather.18.cloned.1.call-update) | async-done | bytes 1048592 | tf_op jit(solution)/shard_map/all_gather | solution.py:34
  55.2 119.8 %all-gather.16.cloned.1.call-done = f32[3072,1024]{1,0:T(8,128)} async-done(((f32[3072,256]{1,0:T(8,128)}), f32[3072,1024]{1,0:T(8,128)}) %all-gather.16.cloned.1.call-update) | async-done | bytes 12582928 | tf_op jit(solution)/shard_map/all_gather | solution.py:33
  175.0 13.8 fusion.28
  188.8 63.4 %while.24 = (s32[]{:T(128)}, f32[8,4,256,8]{2,3,1,0:T(8,128)}, f32[8,4,256]{2,1,0:T(4,128)}, s32[8,4,3072]{2,1,0:T(4,128)S(1)}, f32[8,4,3072,8]{2,3,1,0:T(8,128)S(1)}, /*index=5*/s32[]{:T(128)}) while((s32[]{:T(128)}, f32[8,4,256,8]{2,3,1,0:T(8,128)}, f32[8,4,256]{2,1,0:T(4,128)}, s32[8,4,3072]{2,1,0:T(4,128)S(1)}, ...), condition=%wide.region_2.3_spmd.clone, body=%wide.region_0.2_spmd.clone.sunk | while | flops 314571776 | bytes 635989 | solution.py:59
  188.8 2.3 fusion.70
  191.7 5.0 fusion.69
  196.8 2.3 fusion.70
  199.7 5.0 fusion.69
  204.7 2.3 fusion.70
  207.6 5.0 fusion.69
  212.6 2.3 fusion.70
  215.5 5.0 fusion.69
  220.5 2.3 fusion.70
  223.4 5.0 fusion.69
  228.5 2.3 fusion.70
  231.3 5.0 fusion.69
  236.4 2.3 fusion.70
  239.3 5.0 fusion.69
  244.3 2.3 fusion.70
  247.2 5.0 fusion.69
  252.2 3.5 copy.22
  255.7 4.6 reshape.46
  261.2 110.3 %all-reduce.1 = f32[32,256]{1,0:T(8,128)S(1)} all-reduce(f32[32,256]{1,0:T(8,128)S(1)} %reshape.47), channel_id=9, replica_groups=mesh['rows'=32,'cols'=4] {'rows'}, use_global_device_ids=true, to_apply=%region_4.5.clone | all-reduce | flops 8192 | bytes 65536
  372.4 1.5 fusion.27
  373.9 40.4 %all-gather.6 = f32[32,1,2048]{2,1,0:T(1,128)S(1)} all-gather(f32[1,1,2048]{2,1,0:T(1,128)S(1)} %fusion.27), channel_id=1, replica_groups=mesh['rows'=32,'cols'=4] {'rows'}, dimensions={0}, use_global_device_ids=true | all-gather | bytes 270336 | tf_op jit(solution)/shard_map/all_gather | solution.py:69
  415.0 3.7 reshape.48
  418.6 2.8 copy.23
  421.4 59.3 %while.25 = (s32[]{:T(128)}, f32[8,4,3072,8]{2,3,1,0:T(8,128)}, s32[8,4,3072]{2,1,0:T(4,128)S(1)}, f32[8,4,256,8]{2,3,1,0:T(8,128)S(1)}, s32[]{:T(128)}) while((s32[]{:T(128)}, f32[8,4,3072,8]{2,3,1,0:T(8,128)}, s32[8,4,3072]{2,1,0:T(4,128)S(1)}, f32[8,4,256,8]{2,3,1,0:T(8,128)S(1)}, s32[]{:T(128)}) %tuple.73), condition=%wide.region_6.7_spmd.clone, body=%wide.region_5.6_spmd.clone.sunk | while | flops 305135616 | bytes 574537 | solution.py:86
  421.4 7.4 fusion.72
  428.9 7.4 fusion.72
  436.3 7.4 fusion.72
  443.7 7.4 fusion.72
  451.1 7.4 fusion.72
  458.5 7.4 fusion.72
  465.9 7.4 fusion.72
  473.3 7.4 fusion.72
  480.7 13.6 convolution_bitcast_fusion
  494.3 1.3 copy.25
  495.7 76.6 %reduce-scatter.4.cloned.1.call-done = f32[32,256]{1,0:T(8,128)} async-done(((f32[1024,256]{1,0:T(8,128)}), f32[32,256]{1,0:T(8,128)}) %reduce-scatter.4.cloned.1.call-update) | async-done | bytes 32784 | tf_op jit(solution)/shard_map/reduce_scatter | solution.py:88
  573.8 62.3 %psum.7 = f32[]{:T(128)} all-reduce(f32[]{:T(128)} %multiply_reduce_fusion), channel_id=1, replica_groups=mesh['rows'=32,'cols'=4] {'rows','cols'}, use_global_device_ids=true, to_apply=%region_9.10 | all-reduce | flops 1 | bytes 8 | tf_op jit(solution)/shard_map/psum | solution.py:91
  637.6 12.0 all_gather.66
  649.5 2.0 fusion.29
  651.6 113.2 %all-gather.20.cloned.1.call-done = f32[32768,256]{1,0:T(8,128)} async-done(((f32[1024,256]{1,0:T(8,128)}), f32[32768,256]{1,0:T(8,128)}) %all-gather.20.cloned.1.call-update) | async-done | bytes 33554448 | tf_op jit(solution)/shard_map/all_gather | solution.py:29
  764.8 11.9 reduce_sum.73
  777.4 12.3 all_gather.69
  789.7 2.0 fusion.30
  792.0 112.6 %all-gather.22.cloned.1.call-done = f32[32768,256]{1,0:T(8,128)} async-done(((f32[1024,256]{1,0:T(8,128)}), f32[32768,256]{1,0:T(8,128)}) %all-gather.22.cloned.1.call-update) | async-done | bytes 33554448 | tf_op jit(solution)/shard_map/all_gather | solution.py:29
  904.6 11.9 reduce_sum.74
  917.1 12.3 all_gather.72
  929.5 2.0 fusion.31
  931.5 112.8 %all-gather.24.cloned.1.call-done = f32[32768,256]{1,0:T(8,128)} async-done(((f32[1024,256]{1,0:T(8,128)}), f32[32768,256]{1,0:T(8,128)}) %all-gather.24.cloned.1.call-update) | async-done | bytes 33554448 | tf_op jit(solution)/shard_map/all_gather | solution.py:29
  1044.3 11.9 reduce_sum.75
  1056.9 12.3 all_gather.75
  1069.2 2.0 fusion.32
  1071.3 112.8 %all-gather.26.cloned.1.call-done = f32[32768,256]{1,0:T(8,128)} async-done(((f32[1024,256]{1,0:T(8,128)}), f32[32768,256]{1,0:T(8,128)}) %all-gather.26.cloned.1.call-update) | async-done | bytes 33554448 | tf_op jit(solution)/shard_map/all_gather | solution.py:29
  1184.1 11.9 reduce_sum.76
  1196.6 12.3 all_gather.78
  1209.0 2.0 fusion.33
  1211.0 112.8 %all-gather.28.cloned.1.call-done = f32[32768,256]{1,0:T(8,128)} async-done(((f32[1024,256]{1,0:T(8,128)}), f32[32768,256]{1,0:T(8,128)}) %all-gather.28.cloned.1.call-update) | async-done | bytes 33554448 | tf_op jit(solution)/shard_map/all_gather | solution.py:29
  1323.9 11.9 reduce_sum.77
  1336.4 12.3 all_gather.81
  1348.7 2.0 fusion.34
  1351.5 112.1 %all-gather.30.cloned.1.call-done = f32[32768,256]{1,0:T(8,128)} async-done(((f32[1024,256]{1,0:T(8,128)}), f32[32768,256]{1,0:T(8,128)}) %all-gather.30.cloned.1.call-update) | async-done | bytes 33554448 | tf_op jit(solution)/shard_map/all_gather | solution.py:29
  1463.6 11.9 reduce_sum.78
  (69 shorter events, 17.5 us)
Async XLA Ops:
  7.2 48.0 %all-gather.18.cloned.1.call-start = ((), (), s32[]{:S(2)}) async-start(), calls=%async_computation.2 | async-start | bytes 1081344 | tf_op jit(solution)/shard_map/all_gather | solution.py:34
  7.9 167.1 %all-gather.16.cloned.1.call-start = ((), (), s32[]{:S(2)}) async-start(), calls=%async_computation.1 | async-start | bytes 15728640 | tf_op jit(solution)/shard_map/all_gather | solution.py:33
  8.6 363.7 %all-reduce.4.cloned.1.call-start = ((), (), s32[]{:S(2)}) async-start(), calls=%async_computation.10 | async-start | bytes 524288
  252.2 8.2 copy-start.1
  252.2 8.9 copy-start
  260.4 311.9 %reduce-scatter.4.cloned.1.call-start = ((), (), s32[]{:S(2)}) async-start(), calls=%async_computation.9 | async-start | bytes 1081344 | tf_op jit(solution)/shard_map/reduce_scatter | solution.py:88
  495.7 269.2 %all-gather.20.cloned.1.call-start = ((), (), s32[]{:S(2)}) async-start(), calls=%async_computation.3 | async-start | bytes 34603008 | tf_op jit(solution)/shard_map/all_gather | solution.py:29
  651.6 253.0 %all-gather.22.cloned.1.call-start = ((), (), s32[]{:S(2)}) async-start(), calls=%async_computation.4 | async-start | bytes 34603008 | tf_op jit(solution)/shard_map/all_gather | solution.py:29
  791.7 252.6 %all-gather.24.cloned.1.call-start = ((), (), s32[]{:S(2)}) async-start(), calls=%async_computation.5 | async-start | bytes 34603008 | tf_op jit(solution)/shard_map/all_gather | solution.py:29
  931.5 252.6 %all-gather.26.cloned.1.call-start = ((), (), s32[]{:S(2)}) async-start(), calls=%async_computation.6 | async-start | bytes 34603008 | tf_op jit(solution)/shard_map/all_gather | solution.py:29
  1071.2 252.6 %all-gather.28.cloned.1.call-start = ((), (), s32[]{:S(2)}) async-start(), calls=%async_computation.7 | async-start | bytes 34603008 | tf_op jit(solution)/shard_map/all_gather | solution.py:29
  1211.0 252.6 %all-gather.30.cloned.1.call-start = ((), (), s32[]{:S(2)}) async-start(), calls=%async_computation.8 | async-start | bytes 34603008 | tf_op jit(solution)/shard_map/all_gather | solution.py:29
Sparse Core Ops, SparseCore 0:
  10.3 44.8 all-gather.17
  56.8 118.0 all-gather.15
  260.5 103.2 all-reduce.3
  495.8 76.4 reduce-scatter.3
  651.7 113.0 all-gather.19
  791.9 112.6 all-gather.21
  931.6 112.6 all-gather.23
  1071.4 112.6 all-gather.25
  1211.1 112.6 all-gather.27
  1350.9 112.6 all-gather.29
